TPU v7x, 128 devices: a whole 4x4x4 slice. The times are simulated.
128 devices in a mesh: rows: 16 (over z_lo, x, core), cols: 8 (over z_hi, y).
Axes of the slice: x: 4, y: 4, z: 4 (z_hi: 2, z_lo: 2; z = z_hi * 2 + z_lo), core: 2. Of those that a mesh axis runs over, the one named last changes fastest.
Arguments:
- spectrum: bfloat16 [2, 4096, 4096], P(None, 'rows', 'cols'), may hold values from -6 to 6
- diffraction: bfloat16 [2, 32, 3, 128, 128], P(None, 'rows'), may hold values from -0.21875 to 0.21875
- order_mask: int32 [32, 3], P('rows'), may hold values from 0 to 1, as said below
- phases: float32 [2, 4096, 4096], P(None, 'rows', 'cols'), may hold values from -3.140625 to 3.140625
- transmission: float32 [4096, 4096], P('rows', 'cols'), may hold values from 0.2 to 1
- shifts: int32 [2], replicated, may hold values from 128 to 256, as said below
Outputs:
- outgoing: float32 [2, 4096, 4096], P(None, 'rows', 'cols')
Inputs may be any that keep to these rules, and one draw needn't show every extreme that they name: Each bounce's shift lies between 128 and 256; one bounce shifts by exactly 256. `order_mask`: every block carries the orders -1 and +1; the order 0 is off in some blocks.
All inputs are finite; a program needn't handle non-finite values.
Results may differ from a plain program's by a relative error of at most 0.018.
Values may be sent and summed in bfloat16 or wider, within the bound.
A program may use at most 128 MiB of HBM per device.

v0:
```python
import math
import jax
import jax.numpy as jnp
from jax import lax
from jax.sharding import PartitionSpec as P

BLOCK = 128
BASE = 256
BOUNCES = 2


def shifted(value, axis, steps):
    count = lax.axis_size(axis)
    first, last = (max(0, -steps), min(count, count - steps))
    return lax.ppermute(value, axis, [(source, source + steps) for source in range(first, last)])


def twiddles(extent, sign_value, left_index, right_index):
    wrapped = left_index[:, None] * right_index[None, :] % extent
    angles = wrapped.astype(jnp.float32) * (2.0 * math.pi / extent)
    return (jnp.cos(angles), sign_value * jnp.sin(angles))


def base_tables(target, extent, sign_value):
    turn_real, turn_imag = twiddles(extent, sign_value, jnp.arange(BASE, dtype=jnp.int32), target)
    factor = 1.0 / math.sqrt(extent)
    return ((turn_real * factor).astype(jnp.bfloat16), (turn_imag * factor).astype(jnp.bfloat16))


def blocked_dft(values, axis_at, sign_value, target, extent):
    block_count = values.shape[axis_at] // BASE
    base_real, base_imag = base_tables(target, extent, sign_value)
    if axis_at == 1:
        shaped = values.reshape(2, block_count, BASE, values.shape[2])
        form_text = "sio,ik->sko"
    else:
        shaped = values.reshape(2, values.shape[1], block_count, BASE)
        form_text = "osi,ik->sok"

    def contract(left_side, right_side):
        return jnp.einsum(form_text, left_side, right_side, preferred_element_type=jnp.float32)

    inner_real = contract(shaped[0], base_real) - contract(shaped[1], base_imag)
    inner_imag = contract(shaped[0], base_imag) + contract(shaped[1], base_real)
    numbers = jnp.arange(block_count, dtype=jnp.int32) * BASE
    turn_real, turn_imag = twiddles(extent, sign_value, numbers, target)
    if axis_at == 1:
        turn_real = turn_real[:, :, None]
        turn_imag = turn_imag[:, :, None]
    else:
        turn_real = turn_real[:, None, :]
        turn_imag = turn_imag[:, None, :]
    out_real = jnp.sum(turn_real * inner_real - turn_imag * inner_imag, axis=0)
    out_imag = jnp.sum(turn_real * inner_imag + turn_imag * inner_real, axis=0)
    return jnp.stack([out_real, out_imag])


def apply_blocks(left_side, right_side):
    return jnp.einsum("bjk,bkq->bjq", left_side, right_side, preferred_element_type=jnp.float32)


def diffract(current, offset_step, matrices, weights):
    below_rows = shifted(current, "rows", 1)
    above_rows = shifted(current, "rows", -1)
    widened = jnp.concatenate([below_rows, current, above_rows], axis=1)
    height = current.shape[1]
    columns = current.shape[2]
    block_count = height // BLOCK
    result_real = jnp.zeros((block_count, BLOCK, columns), jnp.float32)
    result_imag = jnp.zeros((block_count, BLOCK, columns), jnp.float32)
    for order_at in range(3):
        source = lax.dynamic_slice_in_dim(widened, height + (order_at - 1) * offset_step, height, 1)
        source = source.reshape(2, block_count, BLOCK, columns)
        kernel = matrices[:, :, order_at]
        weight_now = weights[:, order_at][:, None, None]
        result_real = result_real + weight_now * (
            apply_blocks(kernel[0], source[0]) - apply_blocks(kernel[1], source[1])
        )
        result_imag = result_imag + weight_now * (
            apply_blocks(kernel[0], source[1]) + apply_blocks(kernel[1], source[0])
        )
    return (result_real.reshape(height, columns), result_imag.reshape(height, columns))


def on_device(spectrum, diffraction, order_mask, phases, transmission, shifts):
    local_rows = spectrum.shape[1]
    local_cols = spectrum.shape[2]
    row_count = lax.axis_size("rows")
    col_count = lax.axis_size("cols")
    full_rows = local_rows * row_count
    full_cols = local_cols * col_count
    own_rows = lax.axis_index("rows") * local_rows + jnp.arange(local_rows, dtype=jnp.int32)
    own_cols = lax.axis_index("cols") * local_cols + jnp.arange(local_cols, dtype=jnp.int32)
    weights = order_mask.astype(jnp.float32)

    def rows_gather(values, sign_value):
        summed = blocked_dft(
            lax.all_gather(values, "rows", axis=1, tiled=True), 1, sign_value, own_rows, full_rows
        )
        return summed.astype(jnp.bfloat16)

    def columns_gather(values, sign_value):
        return blocked_dft(
            lax.all_gather(values, "cols", axis=2, tiled=True), 2, sign_value, own_cols, full_cols
        )

    current = spectrum
    outgoing = None
    for bounce in range(BOUNCES):
        closing = bounce == BOUNCES - 1
        diff_real, diff_imag = diffract(current, shifts[bounce], diffraction, weights)
        cosine = jnp.cos(phases[bounce])
        sine_part = jnp.sin(phases[bounce])
        wave_k = jnp.stack(
            [diff_real * cosine - diff_imag * sine_part, diff_real * sine_part + diff_imag * cosine]
        ).astype(jnp.bfloat16)
        rows_space = rows_gather(wave_k, 1.0)
        space = columns_gather(rows_space, 1.0) * transmission[None]
        if closing:
            outgoing = space
        else:
            columns_k = columns_gather(space.astype(jnp.bfloat16), -1.0).astype(jnp.bfloat16)
            current = rows_gather(columns_k, -1.0)
    return outgoing


def solution(mesh):
    placed = (
        P(None, "rows", "cols"),
        P(None, "rows", None, None, None),
        P("rows", None),
        P(None, "rows", "cols"),
        P("rows", "cols"),
        P(),
    )
    return jax.shard_map(
        on_device, mesh=mesh, in_specs=placed, out_specs=P(None, "rows", "cols"), check_vma=False
    )
```

profile of v0, /device:TPU:0, one launch (start us, length us, event | category | flops | bytes accessed | tf_op | source)
XLA Modules:
  0.0 625.4 jit_solution(12232110755991861289)
XLA Ops:
  24.1 58.0 %all-gather.7.cloned.1.call-done = bf16[2,4096,512]{2,1,0:T(8,128)(2,1)} async-done(((bf16[2,256,512]{2,1,0:T(8,128)(2,1)}), bf16[2,4096,512]{2,1,0:T(8,128)(2,1)}) %all-gather.7.cloned.1.call-update) | async-done | bytes 8388624 | tf_op jit(solution)/shard_map/all_gather | solution.py:98
  92.6 6.7 %fusion.21 = (bf16[256,512]{1,0:T(8,128)(2,1)S(1)}, bf16[256,512]{1,0:T(8,128)(2,1)S(1)}) fusion(f32[16,256]{1,0:T(8,128)S(1)} %get-tuple-element.50, f32[16,256]{1,0:T(8,128)S(1)} %get-tuple-element.51, f32[256,16,512]{2,0,1:T(8,128)S(1)} %fusion.109, f32[256,16,512]{2,0,1:T(8,128)S(1)} %fusion.111, f32[256,16,512]{2,0,1:T(8,128)S(1)} %fusion.119, ...), kind=kOutput, calls=%fused_computation.43 | convolution fusion | flops 1095499776 | bytes 29918208 | tf_op jit(solution)/shard_map/sio,ik->sko/dot_general | solution.py:41
  101.6 76.9 %all-gather.9.cloned.1.call-done = bf16[2,256,4096]{2,1,0:T(8,128)(2,1)} async-done(((bf16[2,256,512]{2,1,0:T(8,128)(2,1)}), bf16[2,256,4096]{2,1,0:T(8,128)(2,1)}) %all-gather.9.cloned.1.call-update) | async-done | bytes 4194320 | tf_op jit(solution)/shard_map/all_gather | solution.py:104
  178.4 4.7 fusion.320
  186.4 5.4 fusion.80
  191.8 5.4 fusion.90
  203.8 10.2 %fusion.17 = (f32[256,512]{0,1:T(8,128)S(1)}, f32[256,512]{0,1:T(8,128)S(1)}) fusion(f32[16,512]{1,0:T(8,128)S(1)} %get-tuple-element.47, f32[16,512]{1,0:T(8,128)S(1)} %get-tuple-element.48, f32[512,256,16]{1,0,2:T(8,128)} %fusion.80, f32[512,256,16]{1,0,2:T(8,128)S(1)} %fusion.82, f32[512,256,16]{1,0,2:T(8,128)S(1)} %copy-done.1, ...), kind=kOutput, calls=%fused_computation.35 | convolution fusion | flops 1096548352 | bytes 28379136 | tf_op jit(solution)/shard_map/osi,ik->sok/dot_general | solution.py:41
  215.5 69.9 %all-gather.11.cloned.1.call-done = bf16[2,256,4096]{1,2,0:T(8,128)(2,1)} async-done(((bf16[2,256,512]{1,2,0:T(8,128)(2,1)}), bf16[2,256,4096]{1,2,0:T(8,128)(2,1)}) %all-gather.11.cloned.1.call-update) | async-done | bytes 4194320 | tf_op jit(solution)/shard_map/all_gather | solution.py:104
  297.3 8.7 %fusion.13 = (bf16[256,512]{0,1:T(8,128)(2,1)S(1)}, bf16[256,512]{0,1:T(8,128)(2,1)S(1)}) fusion(f32[16,512]{1,0:T(8,128)S(1)} %get-tuple-element.46, f32[16,512]{1,0:T(8,128)S(1)} %get-tuple-element.48, f32[512,256,16]{1,0,2:T(8,128)S(1)} %fusion.76, f32[512,256,16]{1,0,2:T(8,128)S(1)} %fusion.78, f32[512,256,16]{1,0,2:T(8,128)S(1)} %fusion.94, ...), kind=kOutput, calls=%fused_computation.27 | convolution fusion | flops 1096548352 | bytes 27854848 | tf_op jit(solution)/shard_map/osi,ik->sok/dot_general | solution.py:41
  307.1 58.6 %all-gather.13.cloned.1.call-done = bf16[2,4096,512]{1,2,0:T(8,128)(2,1)} async-done(((bf16[2,256,512]{1,2,0:T(8,128)(2,1)}), bf16[2,4096,512]{1,2,0:T(8,128)(2,1)}) %all-gather.13.cloned.1.call-update) | async-done | bytes 8388624 | tf_op jit(solution)/shard_map/all_gather | solution.py:98
  365.8 6.0 fusion.316
  371.8 6.5 %copy.51 = bf16[1,4096,512]{2,1,0:T(8,128)(2,1)} copy(bf16[1,4096,512]{1,2,0:T(8,128)(2,1)} %get-tuple-element.22) | data formatting | bytes 8388608 | tf_op jit(solution)/shard_map/slice | solution.py:43
  378.2 7.8 %fusion.105 = f32[256,16,512]{2,0,1:T(8,128)} fusion(bf16[16,256,512]{2,1,0:T(8,128)(2,1)} %bitcast.390, s32[256]{0:T(256)S(1)} %copy-done.12), kind=kOutput, calls=%fused_computation.166 | convolution fusion | flops 1074790400 | bytes 12583936 | tf_op jit(solution)/shard_map/sio,ik->sko/dot_general | solution.py:41
  386.0 5.5 fusion.123
  391.5 6.5 %copy.50 = bf16[1,4096,512]{2,1,0:T(8,128)(2,1)} copy(bf16[1,4096,512]{1,2,0:T(8,128)(2,1)} %get-tuple-element.23) | data formatting | bytes 8388608 | tf_op jit(solution)/shard_map/slice | solution.py:43
  398.1 4.6 fusion.107
  404.0 8.0 %fusion.9 = (bf16[256,512]{1,0:T(8,128)(2,1)S(1)}, bf16[256,512]{1,0:T(8,128)(2,1)S(1)}) fusion(f32[16,256]{1,0:T(8,128)S(1)} %copy-done.15, f32[16,256]{1,0:T(8,128)S(1)} %get-tuple-element.51, f32[256,16,512]{2,0,1:T(8,128)} %fusion.105, f32[256,16,512]{2,0,1:T(8,128)S(1)} %fusion.107, f32[256,16,512]{2,0,1:T(8,128)S(1)} %copy-done.4, ...), kind=kOutput, calls=%fused_computation.19 | convolution fusion | flops 1095499776 | bytes 29918208 | tf_op jit(solution)/shard_map/sio,ik->sko/dot_general | solution.py:41
  427.5 57.0 %all-gather.15.cloned.1.call-done = bf16[2,4096,512]{2,1,0:T(8,128)(2,1)} async-done(((bf16[2,256,512]{2,1,0:T(8,128)(2,1)}), bf16[2,4096,512]{2,1,0:T(8,128)(2,1)}) %all-gather.15.cloned.1.call-update) | async-done | bytes 8388624 | tf_op jit(solution)/shard_map/all_gather | solution.py:98
  495.0 6.7 %fusion.5 = (bf16[256,512]{1,0:T(8,128)(2,1)S(1)}, bf16[256,512]{1,0:T(8,128)(2,1)S(1)}) fusion(f32[16,256]{1,0:T(8,128)S(1)} %copy-done.14, f32[16,256]{1,0:T(8,128)S(1)} %get-tuple-element.51, f32[256,16,512]{2,0,1:T(8,128)S(1)} %fusion.101, f32[256,16,512]{2,0,1:T(8,128)S(1)} %fusion.103, f32[256,16,512]{2,0,1:T(8,128)S(1)} %fusion.115, ...), kind=kOutput, calls=%fused_computation.11 | convolution fusion | flops 1095499776 | bytes 29918208 | tf_op jit(solution)/shard_map/sio,ik->sko/dot_general | solution.py:41
  502.5 78.2 %all-gather.17.cloned.1.call-done = bf16[2,256,4096]{2,1,0:T(8,128)(2,1)} async-done(((bf16[2,256,512]{2,1,0:T(8,128)(2,1)}), bf16[2,256,4096]{2,1,0:T(8,128)(2,1)}) %all-gather.17.cloned.1.call-update) | async-done | bytes 4194320 | tf_op jit(solution)/shard_map/all_gather | solution.py:104
  580.8 4.7 fusion.318
  588.7 5.4 fusion.72
  594.1 5.4 fusion.86
  606.4 10.2 %fusion.1 = (f32[256,512]{0,1:T(8,128)S(1)}, f32[256,512]{0,1:T(8,128)S(1)}) fusion(f32[16,512]{1,0:T(8,128)S(1)} %get-tuple-element.47, f32[16,512]{1,0:T(8,128)S(1)} %get-tuple-element.48, f32[512,256,16]{1,0,2:T(8,128)} %fusion.72, f32[512,256,16]{1,0,2:T(8,128)S(1)} %fusion.74, f32[512,256,16]{1,0,2:T(8,128)S(1)} %copy-done, ...), kind=kOutput, calls=%fused_computation.3 | convolution fusion | flops 1096548352 | bytes 28379136 | tf_op jit(solution)/shard_map/osi,ik->sok/dot_general | solution.py:41
  (135 shorter events, 89.9 us)
Async XLA Ops:
  6.5 11.6 %copy-start.6 = (bf16[2,256,512]{2,1,0:T(8,128)(2,1)S(1)}, bf16[2,256,512]{2,1,0:T(8,128)(2,1)}, u32[]{:S(2)}) copy-start(bf16[2,256,512]{2,1,0:T(8,128)(2,1)} %param.6) | copy-start | bytes 1572868
  6.5 11.3 %copy-start.5 = (bf16[2,2,3,128,128]{4,3,2,1,0:T(8,128)(2,1)S(1)}, bf16[2,2,3,128,128]{4,3,2,1,0:T(8,128)(2,1)}, u32[]{:S(2)}) copy-start(bf16[2,2,3,128,128]{4,3,2,1,0:T(8,128)(2,1)} %param.7) | copy-start | bytes 1179652
  6.5 75.5 %all-gather.7.cloned.1.call-start = ((), (), s32[]{:S(2)}) async-start(), calls=%async_computation | async-start | bytes 8912896 | tf_op jit(solution)/shard_map/all_gather | solution.py:98
  6.5 11.5 %collective-permute-start = (bf16[2,256,512]{2,1,0:T(8,128)(2,1)}, bf16[2,256,512]{2,1,0:T(8,128)(2,1)S(1)}, u32[]{:S(2)}, u32[]{:S(2)}) collective-permute-start(bf16[2,256,512]{2,1,0:T(8,128)(2,1)} %param.6), channel_id=1, source_target_pairs={{0,8},{8,16},{16,24},{24,32},{32,40},{40,48},{48,56},{56,64},{64,7... | collective-permute-start | bytes 1572872 | tf_op jit(solution)/shard_map/ppermute | solution.py:15
  8.0 10.2 %collective-permute-start.1 = (bf16[2,256,512]{2,1,0:T(8,128)(2,1)}, bf16[2,256,512]{2,1,0:T(8,128)(2,1)S(1)}, u32[]{:S(2)}, u32[]{:S(2)}) collective-permute-start(bf16[2,256,512]{2,1,0:T(8,128)(2,1)} %param.6), channel_id=1, source_target_pairs={{8,0},{16,8},{24,16},{32,24},{40,32},{48,40},{56,48},{64,56},{72,6... | collective-permute-start | bytes 1572872 | tf_op jit(solution)/shard_map/ppermute | solution.py:15
  11.3 7.2 %copy-start.16 = (f32[2]{0:T(128)}, f32[2]{0:T(128)S(1)}, u32[]{:S(2)}) copy-start(f32[2]{0:T(128)S(1)} %get-tuple-element.18) | copy-start | bytes 28
  11.3 8.3 %copy-start.18 = (f32[2]{0:T(128)}, f32[2]{0:T(128)S(1)}, u32[]{:S(2)}) copy-start(f32[2]{0:T(128)S(1)} %get-tuple-element.19) | copy-start | bytes 28
  11.3 8.8 %copy-start.20 = (f32[2]{0:T(128)}, f32[2]{0:T(128)S(1)}, u32[]{:S(2)}) copy-start(f32[2]{0:T(128)S(1)} %get-tuple-element.17) | copy-start | bytes 28
  23.2 155.2 %all-gather.9.cloned.1.call-start = ((), (), s32[]{:S(2)}) async-start(), calls=%async_computation.1 | async-start | bytes 4718592 | tf_op jit(solution)/shard_map/all_gather | solution.py:104
  23.3 62.6 %copy-start.22 = (s32[16]{0:T(128)}, s32[16]{0:T(128)S(1)}, u32[]{:S(2)}) copy-start(s32[16]{0:T(128)S(1)} %iota_multiply_fusion) | copy-start | bytes 196
  23.3 69.3 %copy-start.11 = (s32[256]{0:T(256)}, s32[256]{0:T(256)S(1)}, u32[]{:S(2)}) copy-start(s32[256]{0:T(256)S(1)} %iota_add_fusion.1) | copy-start | bytes 3076
  24.1 68.5 %copy-start.13 = (f32[16,256]{1,0:T(8,128)}, f32[16,256]{1,0:T(8,128)S(1)}, u32[]{:S(2)}) copy-start(f32[16,256]{1,0:T(8,128)S(1)} %get-tuple-element.50) | copy-start | bytes 49156
  92.6 7.9 %copy-start.9 = (f32[256,512]{1,0:T(8,128)S(1)}, f32[256,512]{1,0:T(8,128)}, u32[]{:S(2)}) copy-start(f32[256,512]{1,0:T(8,128)} %param.10) | copy-start | bytes 1572868
  100.2 185.2 %all-gather.11.cloned.1.call-start = ((), (), s32[]{:S(2)}) async-start(), calls=%async_computation.2 | async-start | bytes 4718592 | tf_op jit(solution)/shard_map/all_gather | solution.py:104
  215.0 150.8 %all-gather.13.cloned.1.call-start = ((), (), s32[]{:S(2)}) async-start(), calls=%async_computation.3 | async-start | bytes 8912896 | tf_op jit(solution)/shard_map/all_gather | solution.py:98
  306.9 177.5 %all-gather.15.cloned.1.call-start = ((), (), s32[]{:S(2)}) async-start(), calls=%async_computation.4 | async-start | bytes 8912896 | tf_op jit(solution)/shard_map/all_gather | solution.py:98
  371.8 6.5 %copy-start.12 = (s32[256]{0:T(256)S(1)}, s32[256]{0:T(256)}, u32[]{:S(2)}) copy-start(s32[256]{0:T(256)} %copy-done.11) | copy-start | bytes 3076
  378.2 7.8 %copy-start.2 = (bf16[1,4096,512]{2,1,0:T(8,128)(2,1)S(1)}, bf16[1,4096,512]{2,1,0:T(8,128)(2,1)}, u32[]{:S(2)}) copy-start(bf16[1,4096,512]{2,1,0:T(8,128)(2,1)} %copy.51) | copy-start | bytes 12582916
  391.5 11.1 %copy-start.15 = (f32[16,256]{1,0:T(8,128)S(1)}, f32[16,256]{1,0:T(8,128)}, u32[]{:S(2)}) copy-start(f32[16,256]{1,0:T(8,128)} %get-tuple-element.49) | copy-start | bytes 49156
  398.0 4.6 copy-start.3
  398.0 5.9 copy-start.4
  412.0 7.5 %collective-permute-start.3 = (bf16[2,256,512]{2,1,0:T(8,128)(2,1)S(1)}, bf16[2,256,512]{2,1,0:T(8,128)(2,1)S(1)}, u32[]{:S(2)}, u32[]{:S(2)}) collective-permute-start(bf16[2,256,512]{2,1,0:T(8,128)(2,1)S(1)} %pad_maximum_fusion.4), channel_id=1, source_target_pairs={{8,0},{16,8},{24,16},{32,24},{40,32},{48,40},{56,48},{64,56},{72,6... | collective-permute-start | bytes 1572872 | tf_op jit(solution)/shard_map/ppermute | solution.py:15
  413.3 7.0 %collective-permute-start.2 = (bf16[2,256,512]{2,1,0:T(8,128)(2,1)S(1)}, bf16[2,256,512]{2,1,0:T(8,128)(2,1)}, u32[]{:S(2)}, u32[]{:S(2)}) collective-permute-start(bf16[2,256,512]{2,1,0:T(8,128)(2,1)S(1)} %pad_maximum_fusion.4), channel_id=1, source_target_pairs={{0,8},{8,16},{16,24},{24,32},{32,40},{40,48},{48,56},{56,64},{64,7... | collective-permute-start | bytes 1572872 | tf_op jit(solution)/shard_map/ppermute | solution.py:15
  427.2 153.6 %all-gather.17.cloned.1.call-start = ((), (), s32[]{:S(2)}) async-start(), calls=%async_computation.5 | async-start | bytes 4718592 | tf_op jit(solution)/shard_map/all_gather | solution.py:104
  (9 other events, 18.7 us)
Sparse Core Ops, SparseCore 0:
  23.3 58.6 all-gather.6
  100.3 78.0 all-gather.8
  215.1 70.2 all-gather.10
  307.0 58.6 all-gather.12
  427.3 57.0 all-gather.14
  502.7 78.0 all-gather.16
where the time goes:
time: 635 us; the launch traced here: 625 us
  waiting for transfers between devices  399 us (63%)
  matrix products  127 us (20%)
  local copies, waits for them, and re-layouts  59.3 us (9%)
  between operations  18.5 us (3%)
  other arithmetic  13 us (2%)
  starting transfers between devices  9.08 us (1%)
    all_gather x3, waiting for transfers between devices, columns_gather(): lax.all_gather(values, 'cols', axis=2, tiled=True)  225 us
    all_gather x3, waiting for transfers between devices, rows_gather(): lax.all_gather(values, 'rows', axis=1, tiled=True)  174 us
    dot_general x24, matrix products, contract(): jnp.einsum(form_text, left_side, right_side, preferred_element_type=jnp.f...  119 us
    slice x12, local copies, waits for them, and re-layouts, blocked_dft(): inner_real = contract(shaped[0], base_real) - contract(shaped[1], base_imag)  51.6 us
  transfers between devices with their start and end apart: 10, of which 6 were waited for; matrix products, arithmetic and copies ran while one was open for 1% of the time, Pallas kernels for 0%

commit v1 on v0

--- a/solution.py
+++ b/solution.py
@@ -100,9 +100,16 @@
         return summed.astype(jnp.bfloat16)
 
     def columns_gather(values, sign_value):
-        return blocked_dft(
-            lax.all_gather(values, "cols", axis=2, tiled=True), 2, sign_value, own_cols, full_cols
+        _name_surface = lambda local_array, shard_axis, array_axis: jnp.concatenate(
+            jax.lax.all_to_all(
+                jnp.stack([local_array for _ in range(jax.lax.psum(1, shard_axis))], 0),
+                shard_axis,
+                0,
+                0,
+            ),
+            array_axis,
         )
+        return blocked_dft(_name_surface(values, "cols", 2), 2, sign_value, own_cols, full_cols)
 
     current = spectrum
     outgoing = None

time: 635 us -> 558 us (0.88)
  waiting for transfers between devices: 399 us -> 225 us
  blocking collectives: 0 us -> 126 us
  local copies, waits for them, and re-layouts: 59.3 us -> 40.5 us
  matrix products: 127 us -> 114 us
    all_gather x3 -> x0, waiting for transfers between devices: 225 us -> none  [columns_gather(): lax.all_gather(values, 'cols', axis=2, tiled=True)]
    all_to_all x0 -> x2, blocking collectives: none -> 126 us  [columns_gather(): jax.lax.all_to_all(jnp.stack([local_array for _ in range(jax.lax.psum(1,...]
    all_to_all x0 -> x1, waiting for transfers between devices: none -> 50.7 us  [columns_gather(): jax.lax.all_to_all(jnp.stack([local_array for _ in range(jax.lax.psum(1,...]
    slice x12 -> x8, local copies, waits for them, and re-layouts: 51.6 us -> 27.5 us  [blocked_dft(): inner_real = contract(shaped[0], base_real) - contract(shaped[1], base_imag)]
    dot_general x24, matrix products: 119 us -> 106 us  [contract(): jnp.einsum(form_text, left_side, right_side, preferred_element_type=jnp.f...]
    all_to_all x0 -> x1, starting transfers between devices: none -> 6.86 us  [columns_gather(): jax.lax.all_to_all(jnp.stack([local_array for _ in range(jax.lax.psum(1,...]
  transfers between devices with their start and end apart: 10 -> 8, of which waited for: 6 -> 4; matrix products, arithmetic and copies ran while one was open for 1% -> 1% of each run, Pallas kernels for 0% -> 0%
where the time goes in v1:
time: 558 us; the launch traced here: 548 us
  waiting for transfers between devices  225 us (40%)
  blocking collectives  126 us (23%)
  matrix products  114 us (20%)
  local copies, waits for them, and re-layouts  40.5 us (7%)
  between operations  18 us (3%)
  starting transfers between devices  15.4 us (3%)
  other arithmetic  9.43 us (2%)
    all_gather x3, waiting for transfers between devices, rows_gather(): lax.all_gather(values, 'rows', axis=1, tiled=True)  174 us
    all_to_all x2, blocking collectives, columns_gather(): jax.lax.all_to_all(jnp.stack([local_array for _ in range(jax.lax.psum(1,...  126 us
    dot_general x24, matrix products, contract(): jnp.einsum(form_text, left_side, right_side, preferred_element_type=jnp.f...  106 us
    all_to_all x1, waiting for transfers between devices, columns_gather(): jax.lax.all_to_all(jnp.stack([local_array for _ in range(jax.lax.psum(1,...  50.7 us
    slice x8, local copies, waits for them, and re-layouts, blocked_dft(): inner_real = contract(shaped[0], base_real) - contract(shaped[1], base_imag)  27.5 us
  transfers between devices with their start and end apart: 8, of which 4 were waited for; matrix products, arithmetic and copies ran while one was open for 1% of the time, Pallas kernels for 0%

profile of v1, /device:TPU:0, one launch (start us, length us, event | category | flops | bytes accessed | tf_op | source)
XLA Modules:
  0.0 548.4 jit_solution(13923018174712619399)
XLA Ops:
  23.3 58.7 %all-gather.4.cloned.1.call-done = bf16[2,4096,512]{2,1,0:T(8,128)(2,1)} async-done(((bf16[2,256,512]{2,1,0:T(8,128)(2,1)}), bf16[2,4096,512]{2,1,0:T(8,128)(2,1)}) %all-gather.4.cloned.1.call-update) | async-done | bytes 8388624 | tf_op jit(solution)/shard_map/all_gather | solution.py:98
  82.0 3.8 fusion.317
  92.5 6.4 %fusion.21 = (bf16[256,512]{1,0:T(8,128)(2,1)S(1)}, bf16[256,512]{1,0:T(8,128)(2,1)S(1)}) fusion(f32[16,256]{1,0:T(8,128)S(1)} %get-tuple-element.50, f32[16,256]{1,0:T(8,128)S(1)} %get-tuple-element.51, f32[256,16,512]{2,0,1:T(8,128)S(1)} %fusion.109, f32[256,16,512]{2,0,1:T(8,128)S(1)} %fusion.111, f32[256,16,512]{2,0,1:T(8,128)S(1)} %fusion.119, ...), kind=kOutput, calls=%fused_computation.43 | convolution fusion | flops 1095499776 | bytes 29918208 | tf_op jit(solution)/shard_map/sio,ik->sko/dot_general | solution.py:41
  101.6 6.9 %all-to-all-start = ((bf16[8,2,256,512]{2,3,1,0:T(8,128)(2,1)}), bf16[8,2,256,512]{2,3,1,0:T(8,128)(2,1)}, u32[]{:S(2)}, u32[]{:S(2)}) async-start(bf16[8,2,256,512]{2,3,1,0:T(8,128)(2,1)} %stack.109), calls=%async_computation | async-start | bytes 8388608 | tf_op jit(solution)/shard_map/all_to_all | solution.py:104
  109.1 50.7 %all-to-all-done = bf16[8,2,256,512]{2,3,1,0:T(8,128)(2,1)} async-done(((bf16[8,2,256,512]{2,3,1,0:T(8,128)(2,1)}), bf16[8,2,256,512]{2,3,1,0:T(8,128)(2,1)}, u32[]{:S(2)}, u32[]{:S(2)}) %all-to-all-start) | async-done | bytes 4194336 | tf_op jit(solution)/shard_map/all_to_all | solution.py:104
  165.8 3.2 fusion.90
  172.1 8.7 %fusion.17 = (f32[256,512]{0,1:T(8,128)S(1)}, f32[256,512]{0,1:T(8,128)S(1)}) fusion(f32[16,512]{1,0:T(8,128)S(1)} %get-tuple-element.47, f32[16,512]{1,0:T(8,128)S(1)} %get-tuple-element.48, f32[512,256,16]{1,0,2:T(8,128)S(1)} %fusion.80, f32[512,256,16]{1,0,2:T(8,128)S(1)} %fusion.82, f32[512,256,16]{1,0,2:T(8,128)S(1)} %fusion.90, ...), kind=kOutput, calls=%fused_computation.35 | convolution fusion | flops 1096548352 | bytes 28379136 | tf_op jit(solution)/shard_map/osi,ik->sok/dot_general | solution.py:41
  181.3 67.9 %all_to_all.15 = bf16[8,2,256,512]{2,3,1,0:T(8,128)(2,1)S(1)} all-to-all(bf16[8,2,256,512]{2,3,1,0:T(8,128)(2,1)S(1)} %stack.113), channel_id=1, replica_groups=mesh['rows'=16,'cols'=8] {'cols'}, dimensions={0} | all-to-all | bytes 8388608 | tf_op jit(solution)/shard_map/all_to_all | solution.py:104
  259.4 8.7 %fusion.13 = (bf16[256,512]{0,1:T(8,128)(2,1)S(1)}, bf16[256,512]{0,1:T(8,128)(2,1)S(1)}) fusion(f32[16,512]{1,0:T(8,128)S(1)} %get-tuple-element.46, f32[16,512]{1,0:T(8,128)S(1)} %get-tuple-element.48, f32[512,256,16]{1,0,2:T(8,128)S(1)} %fusion.76, f32[512,256,16]{1,0,2:T(8,128)S(1)} %fusion.78, f32[512,256,16]{1,0,2:T(8,128)S(1)} %fusion.94, ...), kind=kOutput, calls=%fused_computation.27 | convolution fusion | flops 1096548352 | bytes 27854848 | tf_op jit(solution)/shard_map/osi,ik->sok/dot_general | solution.py:41
  269.2 57.9 %all-gather.6.cloned.1.call-done = bf16[2,4096,512]{1,2,0:T(8,128)(2,1)} async-done(((bf16[2,256,512]{1,2,0:T(8,128)(2,1)}), bf16[2,4096,512]{1,2,0:T(8,128)(2,1)}) %all-gather.6.cloned.1.call-update) | async-done | bytes 8388624 | tf_op jit(solution)/shard_map/all_gather | solution.py:98
  327.1 5.9 %fusion.316 = (bf16[1,4096,512]{1,2,0:T(8,128)(2,1)}, bf16[1,4096,512]{1,2,0:T(8,128)(2,1)}) fusion(bf16[2,4096,512]{1,2,0:T(8,128)(2,1)} %all-gather.6.cloned.1.call-done), kind=kLoop, calls=%fused_computation.399 | loop fusion | bytes 16777216 | tf_op jit(solution)/shard_map/slice | solution.py:43
  333.0 6.5 %copy.51 = bf16[1,4096,512]{2,1,0:T(8,128)(2,1)} copy(bf16[1,4096,512]{1,2,0:T(8,128)(2,1)} %get-tuple-element.22) | data formatting | bytes 8388608 | tf_op jit(solution)/shard_map/slice | solution.py:43
  339.5 7.8 %fusion.105 = f32[256,16,512]{2,0,1:T(8,128)} fusion(bf16[16,256,512]{2,1,0:T(8,128)(2,1)} %bitcast.399, s32[256]{0:T(256)S(1)} %iota_add_fusion.1), kind=kOutput, calls=%fused_computation.169 | convolution fusion | flops 1074790400 | bytes 12583936 | tf_op jit(solution)/shard_map/sio,ik->sko/dot_general | solution.py:41
  347.3 5.5 fusion.123
  352.8 6.5 %copy.50 = bf16[1,4096,512]{2,1,0:T(8,128)(2,1)} copy(bf16[1,4096,512]{1,2,0:T(8,128)(2,1)} %get-tuple-element.23) | data formatting | bytes 8388608 | tf_op jit(solution)/shard_map/slice | solution.py:43
  359.2 4.6 fusion.107
  365.1 8.0 %fusion.9 = (bf16[256,512]{1,0:T(8,128)(2,1)S(1)}, bf16[256,512]{1,0:T(8,128)(2,1)S(1)}) fusion(f32[16,256]{1,0:T(8,128)S(1)} %get-tuple-element.49, f32[16,256]{1,0:T(8,128)S(1)} %get-tuple-element.51, f32[256,16,512]{2,0,1:T(8,128)} %fusion.105, f32[256,16,512]{2,0,1:T(8,128)S(1)} %fusion.107, f32[256,16,512]{2,0,1:T(8,128)S(1)} %copy-done.2, ...), kind=kOutput, calls=%fused_computation.19 | convolution fusion | flops 1095499776 | bytes 29918208 | tf_op jit(solution)/shard_map/sio,ik->sko/dot_general | solution.py:41
  374.5 4.0 collective-permute-start.2
  387.6 57.9 %all-gather.8.cloned.1.call-done = bf16[2,4096,512]{2,1,0:T(8,128)(2,1)} async-done(((bf16[2,256,512]{2,1,0:T(8,128)(2,1)}), bf16[2,4096,512]{2,1,0:T(8,128)(2,1)}) %all-gather.8.cloned.1.call-update) | async-done | bytes 8388624 | tf_op jit(solution)/shard_map/all_gather | solution.py:98
  445.5 3.8 fusion.315
  456.0 6.4 %fusion.5 = (bf16[256,512]{1,0:T(8,128)(2,1)S(1)}, bf16[256,512]{1,0:T(8,128)(2,1)S(1)}) fusion(f32[16,256]{1,0:T(8,128)S(1)} %get-tuple-element.50, f32[16,256]{1,0:T(8,128)S(1)} %get-tuple-element.51, f32[256,16,512]{2,0,1:T(8,128)S(1)} %fusion.101, f32[256,16,512]{2,0,1:T(8,128)S(1)} %fusion.103, f32[256,16,512]{2,0,1:T(8,128)S(1)} %fusion.115, ...), kind=kOutput, calls=%fused_computation.11 | convolution fusion | flops 1095499776 | bytes 29918208 | tf_op jit(solution)/shard_map/sio,ik->sko/dot_general | solution.py:41
  463.0 58.1 %all_to_all.16 = bf16[8,2,256,512]{2,3,1,0:T(8,128)(2,1)S(1)} all-to-all(bf16[8,2,256,512]{2,3,1,0:T(8,128)(2,1)S(1)} %stack.124), channel_id=1, replica_groups=mesh['rows'=16,'cols'=8] {'cols'}, dimensions={0} | all-to-all | bytes 8388608 | tf_op jit(solution)/shard_map/all_to_all | solution.py:104
  525.0 3.2 fusion.86
  531.3 8.7 %fusion.1 = (f32[256,512]{0,1:T(8,128)S(1)}, f32[256,512]{0,1:T(8,128)S(1)}) fusion(f32[16,512]{1,0:T(8,128)S(1)} %get-tuple-element.47, f32[16,512]{1,0:T(8,128)S(1)} %get-tuple-element.48, f32[512,256,16]{1,0,2:T(8,128)S(1)} %fusion.72, f32[512,256,16]{1,0,2:T(8,128)S(1)} %fusion.74, f32[512,256,16]{1,0,2:T(8,128)S(1)} %fusion.86, ...), kind=kOutput, calls=%fused_computation.3 | convolution fusion | flops 1096548352 | bytes 28379136 | tf_op jit(solution)/shard_map/osi,ik->sok/dot_general | solution.py:41
  (102 shorter events, 71.1 us)
Async XLA Ops:
  6.5 11.5 %copy-start.4 = (bf16[2,256,512]{2,1,0:T(8,128)(2,1)S(1)}, bf16[2,256,512]{2,1,0:T(8,128)(2,1)}, u32[]{:S(2)}) copy-start(bf16[2,256,512]{2,1,0:T(8,128)(2,1)} %param.6) | copy-start | bytes 1572868
  6.5 11.2 %copy-start.3 = (bf16[2,2,3,128,128]{4,3,2,1,0:T(8,128)(2,1)S(1)}, bf16[2,2,3,128,128]{4,3,2,1,0:T(8,128)(2,1)}, u32[]{:S(2)}) copy-start(bf16[2,2,3,128,128]{4,3,2,1,0:T(8,128)(2,1)} %param.7) | copy-start | bytes 1179652
  6.5 75.5 %all-gather.4.cloned.1.call-start = ((), (), s32[]{:S(2)}) async-start(), calls=%async_computation.3 | async-start | bytes 8912896 | tf_op jit(solution)/shard_map/all_gather | solution.py:98
  6.5 11.4 %collective-permute-start = (bf16[2,256,512]{2,1,0:T(8,128)(2,1)}, bf16[2,256,512]{2,1,0:T(8,128)(2,1)S(1)}, u32[]{:S(2)}, u32[]{:S(2)}) collective-permute-start(bf16[2,256,512]{2,1,0:T(8,128)(2,1)} %param.6), channel_id=1, source_target_pairs={{0,8},{8,16},{16,24},{24,32},{32,40},{40,48},{48,56},{56,64},{64,7... | collective-permute-start | bytes 1572872 | tf_op jit(solution)/shard_map/ppermute | solution.py:15
  8.0 10.1 %collective-permute-start.1 = (bf16[2,256,512]{2,1,0:T(8,128)(2,1)}, bf16[2,256,512]{2,1,0:T(8,128)(2,1)S(1)}, u32[]{:S(2)}, u32[]{:S(2)}) collective-permute-start(bf16[2,256,512]{2,1,0:T(8,128)(2,1)} %param.6), channel_id=1, source_target_pairs={{8,0},{16,8},{24,16},{32,24},{40,32},{48,40},{56,48},{64,56},{72,6... | collective-permute-start | bytes 1572872 | tf_op jit(solution)/shard_map/ppermute | solution.py:15
  19.0 1.2 copy-start.5
  101.6 7.1 %copy-start.6 = (f32[256,512]{1,0:T(8,128)S(1)}, f32[256,512]{1,0:T(8,128)}, u32[]{:S(2)}) copy-start(f32[256,512]{1,0:T(8,128)} %param.10) | copy-start | bytes 1572868
  101.6 58.2 %all-to-all-start = ((bf16[8,2,256,512]{2,3,1,0:T(8,128)(2,1)}), bf16[8,2,256,512]{2,3,1,0:T(8,128)(2,1)}, u32[]{:S(2)}, u32[]{:S(2)}) async-start(bf16[8,2,256,512]{2,3,1,0:T(8,128)(2,1)} %stack.109), calls=%async_computation | async-start | bytes 8388608 | tf_op jit(solution)/shard_map/all_to_all | solution.py:104
  108.4 218.7 %all-gather.6.cloned.1.call-start = ((), (), s32[]{:S(2)}) async-start(), calls=%async_computation.4 | async-start | bytes 8912896 | tf_op jit(solution)/shard_map/all_gather | solution.py:98
  269.0 176.5 %all-gather.8.cloned.1.call-start = ((), (), s32[]{:S(2)}) async-start(), calls=%async_computation.5 | async-start | bytes 8912896 | tf_op jit(solution)/shard_map/all_gather | solution.py:98
  339.5 7.8 %copy-start = (bf16[1,4096,512]{2,1,0:T(8,128)(2,1)S(1)}, bf16[1,4096,512]{2,1,0:T(8,128)(2,1)}, u32[]{:S(2)}) copy-start(bf16[1,4096,512]{2,1,0:T(8,128)(2,1)} %copy.51) | copy-start | bytes 12582916
  359.2 4.6 copy-start.1
  359.2 5.9 %copy-start.2 = (f32[256,16,512]{2,0,1:T(8,128)S(1)}, f32[256,16,512]{2,0,1:T(8,128)}, u32[]{:S(2)}) copy-start(f32[256,16,512]{2,0,1:T(8,128)} %fusion.123) | copy-start | bytes 25165828
  373.2 7.7 %collective-permute-start.3 = (bf16[2,256,512]{2,1,0:T(8,128)(2,1)S(1)}, bf16[2,256,512]{2,1,0:T(8,128)(2,1)}, u32[]{:S(2)}, u32[]{:S(2)}) collective-permute-start(bf16[2,256,512]{2,1,0:T(8,128)(2,1)S(1)} %pad_maximum_fusion.4), channel_id=1, source_target_pairs={{8,0},{16,8},{24,16},{32,24},{40,32},{48,40},{56,48},{64,56},{72,6... | collective-permute-start | bytes 1572872 | tf_op jit(solution)/shard_map/ppermute | solution.py:15
  374.5 6.4 %collective-permute-start.2 = (bf16[2,256,512]{2,1,0:T(8,128)(2,1)S(1)}, bf16[2,256,512]{2,1,0:T(8,128)(2,1)}, u32[]{:S(2)}, u32[]{:S(2)}) collective-permute-start(bf16[2,256,512]{2,1,0:T(8,128)(2,1)S(1)} %pad_maximum_fusion.4), channel_id=1, source_target_pairs={{0,8},{8,16},{16,24},{24,32},{32,40},{40,48},{48,56},{56,64},{64,7... | collective-permute-start | bytes 1572872 | tf_op jit(solution)/shard_map/ppermute | solution.py:15
Sparse Core Ops, SparseCore 0:
  23.2 58.7 all-gather.3
  269.1 57.9 all-gather.5
  387.7 57.7 all-gather.7
